TPU v7x, 512 devices: a whole 4x8x8 slice. The times are simulated.
512 devices in a mesh: var: 16 (over x, y_hi, core), tm: 32 (over z, y_lo).
Axes of the slice: x: 4, y: 8 (y_hi: 2, y_lo: 4; y = y_hi * 4 + y_lo), z: 8, core: 2. Of those that a mesh axis runs over, the one named last changes fastest.
Arguments:
- latent: bfloat16 [16, 8192, 1536], P('var', 'tm')
- fresh_noise: bfloat16 [16, 8192, 1536], P('var', 'tm'), may hold values from -6 to 6
- timestep: int32 [1], replicated, may hold values from 400 to 800
- prompt_ids: int32 [16, 64], P('var'), may hold values from 0 to 16383
- block_table: int32 [3, 3], replicated, may hold values from 0 to 1, as said below
- prompt_table: bfloat16 [16384, 1536], P(None, 'tm'), may hold values from -12 to 12
- w_query: bfloat16 [1536, 768], P('var')
- w_keyval: bfloat16 [1536, 1536], P('var')
- w_out: bfloat16 [768, 1536], P('var'), may hold values from -0.4375 to 0.4375
Outputs:
- stepped: bfloat16 [16, 8192, 1536], P('var', 'tm')
Inputs may be any that keep to these rules, and one draw needn't show every extreme that they name: `block_table`: the diagonal and the first column of the table are always 1.
All inputs are finite; a program needn't handle non-finite values.
Results may differ from a plain program's by a relative error of at most 0.0048.
Values may be sent and summed in bfloat16 or wider, within the bound.
A program may use at most 64 MiB of HBM per device.

v0:
```python
import math

import jax
import jax.numpy as jnp
from jax import lax
from jax.sharding import PartitionSpec as P

HEADS = 12
HS = 64
SEAM = 128
BLK = 128
TSTEPS = 1000
STRIDE = 200


epsilon = 1e-06


def shifted(block, axis, distance):
    devices = range(lax.axis_size(axis))
    route = [(i - distance, i) for i in devices if i - distance in devices]
    return lax.ppermute(block, axis, route)


def broadcast(value, axis, source):
    kept = jnp.where(lax.axis_index(axis) == source, value, 0).astype(value.dtype)
    return lax.psum(kept, axis)


def plan(moment):
    return jnp.cos((moment / TSTEPS + 0.008) / 1.008 * (math.pi / 2.0)) ** 2


def coefficients(timestep):
    current = timestep[0].astype(jnp.float32)
    abar_now = plan(current)
    abar_prev = plan(current - STRIDE)
    spread = jnp.sqrt((1.0 - abar_prev) / (1.0 - abar_now) * (1.0 - abar_now / abar_prev))
    carried = jnp.sqrt((1.0 - abar_prev) * (abar_now / abar_prev - abar_now) / (1.0 - abar_now))
    coef_pred = carried - jnp.sqrt(abar_prev) * jnp.sqrt(1.0 - abar_now) / jnp.sqrt(abar_now)
    coef_latent = jnp.sqrt(abar_prev / abar_now)
    return (current, coef_latent, coef_pred, spread)


def time_embedding(current, model_width):
    half_width = model_width // 2
    frequency = jnp.exp(-math.log(10000.0) * jnp.arange(half_width, dtype=jnp.float32) / half_width)
    angles = current * frequency
    return jnp.concatenate([jnp.cos(angles), jnp.sin(angles)])


def attend(queries, keys, values, both_masks):
    window_rows = queries.shape[0]
    key_rows = keys.shape[0]
    query_heads = queries.reshape(window_rows, HEADS, HS).transpose(1, 0, 2)
    key_heads = keys.reshape(key_rows, HEADS, HS).transpose(1, 0, 2)
    value_heads = values.reshape(key_rows, HEADS, HS).transpose(1, 0, 2)

    def one_head(operands):
        head_query, head_key, head_value = operands
        scores = jnp.einsum(
            "qd,kd->qk", head_query, head_key, preferred_element_type=jnp.float32
        ) * (1.0 / math.sqrt(HS))
        scores = jnp.where(both_masks, scores, -1e30)
        row_max = jnp.max(scores, axis=-1, keepdims=True)
        weights = jnp.exp(scores - row_max)
        row_sum = jnp.sum(weights, axis=-1, keepdims=True)
        probs = (weights / row_sum).astype(jnp.bfloat16)
        return jnp.dot(probs, head_value, preferred_element_type=jnp.float32)

    attended = lax.map(one_head, (query_heads, key_heads, value_heads))
    return attended.transpose(1, 0, 2).reshape(window_rows, HEADS * HS)


def local(
    latent, fresh_noise, timestep, prompt_ids, block_table, prompt_table, w_query, w_keyval, w_out
):
    own_rows = latent.shape[1]
    model_width = latent.shape[2]
    head_width = w_query.shape[1]
    tm_count = lax.axis_size("tm")
    tm_place = lax.axis_index("tm")
    current, coef_latent, coef_pred, spread = coefficients(timestep)
    embedded = time_embedding(current, model_width)
    local_pooled = jnp.mean(prompt_table[prompt_ids[0]].astype(jnp.float32), axis=0)
    pooled = lax.all_gather(local_pooled, "tm", axis=0, tiled=True)
    condition = embedded + pooled
    values = latent[0].astype(jnp.float32)
    inv_norm = lax.rsqrt(jnp.mean(values * values, axis=-1, keepdims=True) + epsilon)
    normed = (values * inv_norm * (1.0 + condition[None, :])).astype(jnp.bfloat16)
    window_rows = own_rows + SEAM
    allowed = jnp.repeat(jnp.repeat(block_table, BLK, axis=0), BLK, axis=1) > 0
    key_valid = (jnp.arange(window_rows) < own_rows) | (tm_place != tm_count - 1)
    key_mask = allowed & key_valid[None, :]
    both_masks = jnp.concatenate([key_mask, key_mask], axis=1)
    arrived = shifted(normed[:SEAM], "tm", -1)
    window_inputs = jnp.concatenate([normed, arrived], axis=0)
    columns = window_inputs
    query_sum = jnp.dot(
        columns,
        lax.all_gather(w_query, "var", axis=0, tiled=True),
        preferred_element_type=jnp.float32,
    )
    keyval_sum = jnp.dot(
        columns,
        lax.all_gather(w_keyval, "var", axis=0, tiled=True),
        preferred_element_type=jnp.float32,
    )
    window_query = query_sum.astype(jnp.bfloat16)
    window_keyval = keyval_sum.astype(jnp.bfloat16)
    source_window = broadcast(window_keyval, "var", 0)
    all_keys = jnp.concatenate(
        [window_keyval[:, :head_width], source_window[:, :head_width]], axis=0
    )
    all_values = jnp.concatenate(
        [window_keyval[:, head_width:], source_window[:, head_width:]], axis=0
    )
    attended = attend(window_query, all_keys, all_values, both_masks)
    ramp_up = (jnp.arange(SEAM, dtype=jnp.float32) + 0.5) / SEAM
    tail_part = attended[own_rows:] * (1.0 - ramp_up)[:, None]
    received = shifted(tail_part.astype(jnp.bfloat16), "tm", 1).astype(tail_part.dtype)
    lead_weight = jnp.where(tm_place == 0, 1.0, ramp_up)
    lead_part = attended[:SEAM] * lead_weight[:, None] + received
    blended = jnp.concatenate([lead_part, attended[SEAM:own_rows]], axis=0).astype(jnp.bfloat16)
    columns = blended
    prediction = jnp.dot(
        columns,
        lax.all_gather(w_out, "var", axis=0, tiled=True),
        preferred_element_type=jnp.float32,
    )
    result = (
        coef_latent * values + coef_pred * prediction + spread * fresh_noise[0].astype(jnp.float32)
    )
    return result.astype(jnp.bfloat16)[None]


def solution(mesh):
    placed = (
        P("var", "tm", None),
        P("var", "tm", None),
        P(),
        P("var", None),
        P(),
        P(None, "tm"),
        P("var", None),
        P("var", None),
        P("var", None),
    )
    return jax.shard_map(
        local, mesh=mesh, in_specs=placed, out_specs=P("var", "tm", None), check_vma=False
    )
```

profile of v0, /device:TPU:1, one launch (start us, length us, event | category | flops | bytes accessed | tf_op | source)
XLA Modules:
  0.0 446.6 jit_solution(14416364321004874761)
XLA Ops:
  6.5 0.7 all-gather.6.cloned.1.call-update
  7.3 0.7 all-gather.4.cloned.1.call-update
  8.7 4.9 %copy.14 = bf16[16384,48]{1,0:T(8,128)(2,1)} copy(bf16[16384,48]{0,1:T(8,128)(2,1)} %param.16) | data formatting | bytes 3145728 | tf_op args[5]
  13.6 1.3 dynamic-slice
  15.6 3.3 gather_fusion
  19.0 86.1 %all-reduce = f32[1536]{0:T(1024)S(1)} all-reduce(f32[1536]{0:T(1024)S(1)} %multiply_dynamic-update-slice_fusion), channel_id=1, replica_groups=mesh['var'=16,'tm'=32] {'tm'}, use_global_device_ids=true, to_apply=%add | all-reduce | flops 1536 | bytes 12288
  105.2 0.2 fusion.17
  105.4 0.2 fusion.19
  105.7 1.3 collective-permute-start
  107.0 7.3 %collective-permute-done = bf16[128,1536]{1,0:T(8,128)(2,1)S(1)} collective-permute-done((bf16[128,1536]{1,0:T(8,128)(2,1)S(1)}, bf16[128,1536]{1,0:T(8,128)(2,1)S(1)}, u32[]{:S(2)}, u32[]{:S(2)}) %collective-permute-start) | collective-permute-done | bytes 393248 | tf_op jit(solution)/shard_map/ppermute | solution.py:22
  114.3 5.8 %broadcast_select_fusion = (bf16[384,1536]{1,0:T(8,128)(2,1)}, bf16[384,1536]{1,0:T(8,128)(2,1)}) fusion(pred[]{:T(512)S(6)} %eq.6, bf16[1536,1536]{1,0:T(8,128)(2,1)} %all-gather.6.cloned.1.call-done, bf16[128,1536]{1,0:T(8,128)(2,1)S(1)} %collective-permute-done, bf16[256,1536]{1,0:T(8,128)(2,1)S(1)} %fusion.19), kind=kOutput, calls=%fused_computation.35 | convolution fusion | flops 1815478272 | bytes 8257537 | tf_op jit(solution)/shard_map/dot_general | solution.py:104
  120.2 0.5 all-gather.8.cloned.1.call-update
  121.3 0.4 copy.21
  121.6 50.7 %all-gather.4.cloned.1.call-done = bf16[1536,768]{1,0:T(8,128)(2,1)} async-done(((bf16[96,768]{1,0:T(8,128)(2,1)}), bf16[1536,768]{1,0:T(8,128)(2,1)}) %all-gather.4.cloned.1.call-update) | async-done | bytes 2359312 | tf_op jit(solution)/shard_map/all_gather | solution.py:101
  172.4 2.7 convolution_convert_fusion.1
  175.1 1.1 copy.15
  176.2 0.4 copy-done.2
  176.7 183.7 %all-reduce.3.cloned.1.call-done = bf16[384,1536]{1,0:T(8,128)(2,1)} async-done(((bf16[384,1536]{1,0:T(8,128)(2,1)}), bf16[384,1536]{1,0:T(8,128)(2,1)}) %all-reduce.3.cloned.1.call-update) | async-done | bytes 1179664 | tf_op jit(solution)/shard_map/psum | solution.py:27
  360.3 2.1 fusion.38
  362.6 1.4 copy.18
  364.1 0.6 copy.16
  364.8 43.3 %while.10 = (s32[]{:T(128)}, f32[12,384,64]{1,2,0:T(8,128)}, bf16[12,384,64]{1,2,0:T(8,128)(2,1)}, bf16[12,768,64]{1,2,0:T(8,128)(2,1)S(1)}, pred[384,768]{1,0:T...) while((s32[]{:T(128)}, f32[12,384,64]{1,2,0:T(8,128)}, bf16[12,384,64]{1,2,0:T(8,128)(2,1)}, ...), condition=%wide.region_6.7_spmd, body=%wide.region_3.6_spmd.sunk | while | flops 77856000 | bytes 4187725 | solution.py:71
  364.8 1.3 fusion.47
  366.0 0.3 fusion.48
  366.4 2.0 fusion.49
  368.4 1.3 fusion.47
  369.6 0.3 fusion.48
  370.0 2.0 fusion.49
  372.0 1.3 fusion.47
  373.2 0.3 fusion.48
  373.6 2.0 fusion.49
  375.6 1.3 fusion.47
  376.8 0.3 fusion.48
  377.2 2.0 fusion.49
  379.2 1.3 fusion.47
  380.5 0.3 fusion.48
  380.8 2.0 fusion.49
  382.8 1.3 fusion.47
  384.1 0.4 fusion.48
  384.4 2.0 fusion.49
  386.4 1.3 fusion.47
  387.7 0.3 fusion.48
  388.0 2.0 fusion.49
  390.0 1.3 fusion.47
  391.3 0.3 fusion.48
  391.7 2.0 fusion.49
  393.7 1.3 fusion.47
  394.9 0.3 fusion.48
  395.3 2.0 fusion.49
  397.3 1.3 fusion.47
  398.5 0.3 fusion.48
  398.9 2.0 fusion.49
  400.9 1.3 fusion.47
  402.1 0.3 fusion.48
  402.5 2.0 fusion.49
  404.5 1.3 fusion.47
  405.7 0.3 fusion.48
  406.1 2.0 fusion.49
  408.1 1.2 fusion.36
  409.3 2.4 collective-permute-start.1
  412.3 1.0 slice.56
  413.3 8.1 %collective-permute-done.1 = bf16[128,768]{0,1:T(8,128)(2,1)S(1)} collective-permute-done((bf16[128,768]{0,1:T(8,128)(2,1)S(1)}, bf16[128,768]{0,1:T(8,128)(2,1)S(1)}, u32[]{:S(2)}, u32[]{:S(2)}) %collective-permute-start.1) | collective-permute-done | bytes 196640 | tf_op jit(solution)/shard_map/ppermute | solution.py:22
  421.5 15.2 %all-gather.8.cloned.1.call-done = bf16[768,1536]{1,0:T(8,128)(2,1)} async-done(((bf16[48,1536]{1,0:T(8,128)(2,1)}), bf16[768,1536]{1,0:T(8,128)(2,1)}) %all-gather.8.cloned.1.call-update) | async-done | bytes 2359312 | tf_op jit(solution)/shard_map/all_gather | solution.py:128
  436.6 3.5 fusion.16
  (41 shorter events, 1.2 us)
Async XLA Ops:
  6.5 107.8 %all-gather.6.cloned.1.call-start = ((), (), s32[]{:S(2)}) async-start(), calls=%async_computation.1 | async-start | bytes 5013504 | tf_op jit(solution)/shard_map/all_gather | solution.py:106
  7.3 165.1 %all-gather.4.cloned.1.call-start = ((), (), s32[]{:S(2)}) async-start(), calls=%async_computation | async-start | bytes 2506752 | tf_op jit(solution)/shard_map/all_gather | solution.py:101
  8.0 352.3 %all-reduce.3.cloned.1.call-start = ((), (), s32[]{:S(2)}) async-start(), calls=%async_computation.2 | async-start | bytes 2359296 | tf_op jit(solution)/shard_map/psum | solution.py:27
  8.7 6.8 %copy-start.5 = (s32[1,64]{1,0:T(1,128)S(1)}, s32[1,64]{1,0:T(1,128)}, u32[]{:S(2)}) copy-start(s32[1,64]{1,0:T(1,128)} %param.14) | copy-start | bytes 772
  8.7 96.5 %copy-start = (bf16[1,256,1536]{2,1,0:T(8,128)(2,1)S(1)}, bf16[1,256,1536]{2,1,0:T(8,128)(2,1)}, u32[]{:S(2)}) copy-start(bf16[1,256,1536]{2,1,0:T(8,128)(2,1)} %param.11) | copy-start | bytes 2359300
  105.7 8.6 %collective-permute-start = (bf16[128,1536]{1,0:T(8,128)(2,1)S(1)}, bf16[128,1536]{1,0:T(8,128)(2,1)S(1)}, u32[]{:S(2)}, u32[]{:S(2)}) collective-permute-start(bf16[128,1536]{1,0:T(8,128)(2,1)S(1)} %slice.47), channel_id=1, source_target_pairs={{1,0},{2,1},{3,2},{4,3},{5,4},{6,5},{7,6},{8,7},{9,8},{10,9},{11,1... | collective-permute-start | bytes 1179656 | tf_op jit(solution)/shard_map/ppermute | solution.py:22
  120.1 0.7 copy-start.3
  120.2 316.5 %all-gather.8.cloned.1.call-start = ((), (), s32[]{:S(2)}) async-start(), calls=%async_computation.3 | async-start | bytes 2506752 | tf_op jit(solution)/shard_map/all_gather | solution.py:128
  175.1 1.5 copy-start.2
  362.6 1.5 copy-start.1
  409.3 27.4 %copy-start.4 = (bf16[1,256,1536]{2,1,0:T(8,128)(2,1)S(1)}, bf16[1,256,1536]{2,1,0:T(8,128)(2,1)}, u32[]{:S(2)}) copy-start(bf16[1,256,1536]{2,1,0:T(8,128)(2,1)} %param.12) | copy-start | bytes 2359300
  409.3 12.1 %collective-permute-start.1 = (bf16[128,768]{0,1:T(8,128)(2,1)S(1)}, bf16[128,768]{0,1:T(8,128)(2,1)S(1)}, u32[]{:S(2)}, u32[]{:S(2)}) collective-permute-start(bf16[128,768]{0,1:T(8,128)(2,1)S(1)} %fusion.23), channel_id=1, source_target_pairs={{0,1},{1,2},{2,3},{3,4},{4,5},{5,6},{6,7},{7,8},{8,9},{9,10},{10,1... | collective-permute-start | bytes 589832 | tf_op jit(solution)/shard_map/ppermute | solution.py:22
Sparse Core Ops, SparseCore 0:
  10.6 94.2 all-gather.5
  108.2 64.1 all-gather.3
  175.3 184.9 all-reduce.2
  363.5 73.0 all-gather.7
where the time goes:
time: 449 us; the launch traced here: 447 us
  waiting for transfers between devices  267 us (59%)
  blocking collectives  86.1 us (19%)
  matrix products  51.1 us (11%)
  local copies, waits for them, and re-layouts  18.1 us (4%)
  between operations  15.2 us (3%)
  other arithmetic  5.39 us (1%)
    psum x1, waiting for transfers between devices, broadcast(): return lax.psum(kept, axis)  184 us
    unnamed x1, blocking collectives  86.1 us
    all_gather x1, waiting for transfers between devices, local(): lax.all_gather(w_query, 'var', axis=0, tiled=True)  50.7 us
    dot_general x12, matrix products, one_head(): return jnp.dot(probs, head_value, preferred_element_type=jnp.float32)  24 us
    ppermute x2, waiting for transfers between devices, shifted(): return lax.ppermute(block, axis, route)  15.4 us
    all_gather x1, waiting for transfers between devices, local(): lax.all_gather(w_out, 'var', axis=0, tiled=True)  15.2 us
    dot_general x12, matrix products, one_head(): jnp.einsum('qd,kd->qk', head_query, head_key, preferred_element_type=jnp....  15.1 us
  transfers between devices with their start and end apart: 6, of which 5 were waited for; matrix products, arithmetic and copies ran while one was open for 16% of the time, Pallas kernels for 0%

commit v1 on v0

v1 whole, which is shorter than its diff:
```python
import math

import jax
import jax.numpy as jnp
from jax import lax
from jax.experimental import pallas as pl
from jax.experimental.pallas import tpu as pltpu
from jax.sharding import PartitionSpec as P

MESH = pl.DeviceIdType.MESH
F32 = jnp.float32
BF16 = jnp.bfloat16

D = 1536
HD = 768
CH = 256
SEAM = 128
WIN = CH + SEAM
PROMPT = 64
TSTEPS = 1000
STRIDE = 200
NX, NZ, NL = 4, 8, 4
EPS = 1e-06
QP, KP, VP, OP = 0, 1, 2, 3


def plan(moment):
    return jnp.cos((moment / TSTEPS + 0.008) / 1.008 * (math.pi / 2.0)) ** 2


def coefficients(timestep):
    current = timestep[0].astype(F32)
    abar_now = plan(current)
    abar_prev = plan(current - STRIDE)
    spread = jnp.sqrt((1.0 - abar_prev) / (1.0 - abar_now) * (1.0 - abar_now / abar_prev))
    carried = jnp.sqrt((1.0 - abar_prev) * (abar_now / abar_prev - abar_now) / (1.0 - abar_now))
    coef_pred = carried - jnp.sqrt(abar_prev) * jnp.sqrt(1.0 - abar_now) / jnp.sqrt(abar_now)
    coef_latent = jnp.sqrt(abar_prev / abar_now)
    return (current, coef_latent, coef_pred, spread)


def time_embedding(current):
    half_width = D // 2
    frequency = jnp.exp(-math.log(10000.0) * jnp.arange(half_width, dtype=F32) / half_width)
    angles = current * frequency
    return jnp.concatenate([jnp.cos(angles), jnp.sin(angles)])


def window_tile(tm):
    return min(48 * tm // 128, 10)


def kernel(
    latent, noise, embedded, coefs, block_table, prompt_ids, table, w_query, w_keyval, w_out,
    out,
    wqkv, wo, xw, sp, xn, tabv, counts, mine, pooled, q_s, k_s, v_s, s_s, p_s, blended, tail_out, tail_in, noise_v,
    loc, xs, xr, x2s, x2r, ys, yr, zs, zr, ss, sr,
    s0s, s0r, s1s, s1r, s2s, s2r, s3s, s3r, s4s, s4r, seam_s, seam_r, tail_s, tail_r,
    p0s, p0r, p1s, p1r, p2s, p2r,
):
    var, tm = lax.axis_index("var"), lax.axis_index("tm")
    x, yh, c = var // 4, (var // 2) % 2, var % 2
    z, yl = tm // NL, tm % NL
    par = z % 2
    y = yh * NL + yl
    xm, xp, xq = (x + 3) % NX, (x + 1) % NX, (x + 2) % NX
    y_up, y_dn = (y + 1) % 8, (y + 7) % 8

    def at(x_, yh_, c_, z_, yl_):
        return {"var": (x_ * 2 + yh_) * 2 + c_, "tm": z_ * NL + yl_}

    sib = at(x, yh, 1 - c, z, yl)
    x_left, x_right = at(xm, yh, c, z, yl), at(xp, yh, c, z, yl)
    y_next = at(x, y_up // NL, c, z, y_up % NL)
    y_prev = at(x, y_dn // NL, c, z, y_dn % NL)
    z_next, z_prev = at(x, yh, c, (z + 1) % NZ, yl), at(x, yh, c, (z + 7) % NZ, yl)
    partner = at(x, 1 - yh, c, z, yl)
    tm_next, tm_prev = {"var": var, "tm": (tm + 1) % 32}, {"var": var, "tm": (tm + 31) % 32}
    src_here, src_next = {"var": 0, "tm": tm}, {"var": 0, "tm": (tm + 1) % 32}

    def remote(src, dst, send, recv, device):
        return pltpu.make_async_remote_copy(
            src_ref=src, dst_ref=dst, send_sem=send, recv_sem=recv, device_id=device, device_id_type=MESH
        )

    pending = []

    def send(src, dst, ssem, rsem, device, when=None):
        if when is None:
            remote(src, dst, ssem, rsem, device).start()
        else:
            @pl.when(when)
            def _():
                remote(src, dst, ssem, rsem, device).start()

    def sent(src, ssem, when=None):
        pending.append((src, ssem, when))

    def arrived(dst, rsem):
        remote(dst, dst, rsem, rsem, sib).wait_recv()

    barrier = pltpu.get_barrier_semaphore()

    def greet(device):
        pl.semaphore_signal(barrier, inc=1, device_id=device, device_id_type=MESH)

    for device in (x_left, x_right, sib, y_next, y_prev, partner, tm_next, tm_prev, src_next):
        greet(device)
    for k in range(1, NZ):
        greet(at(x, yh, c, (z + k) % NZ, yl))
    for k in range(1, NL):
        greet(at(x, yh, c, z, (yl + k) % NL))

    @pl.when(var != 0)
    def _():
        greet(src_here)

    own = x * 2 + yh
    lats = latent.at[0]
    inputs = (w_query, w_keyval.at[:, pl.ds(0, HD)], w_keyval.at[:, pl.ds(HD, HD)], w_out)

    def full(p, m, cc):
        return wo.at[m, cc] if p == OP else wqkv.at[p, m, cc]

    def x_half(p, m, cc, h):
        return wo.at[m, cc, :, pl.ds(h * 768, 768)] if p == OP else wqkv.at[p, m, cc, pl.ds(h * 48, 48), :]

    def y_blk(p, m, cc, pr, d):
        if p == OP:
            return wo.at[m, cc, :, pl.ds(pl.multiple_of(pr * 768 + d * 384, 128), 384)]
        return wqkv.at[p, m, cc, pl.ds(pl.multiple_of(pr * 48, 16), 48), pl.ds(d * 384, 384)]

    table_in = pltpu.make_async_copy(table, tabv, loc.at[0])
    table_in.start()
    weights_in = [pltpu.make_async_copy(inputs[p], full(p, own, c), loc.at[1 + p]) for p in range(4)]
    for copy in weights_in:
        copy.start()
    latent_in = pltpu.make_async_copy(lats, xw.at[pl.ds(0, CH)], loc.at[5])
    latent_in.start()
    noise_in = pltpu.make_async_copy(noise.at[0], noise_v, loc.at[6])
    noise_in.start()

    ids = prompt_ids[...]
    rows = lax.broadcasted_iota(jnp.int32, (128, PROMPT), 0)
    high = (rows == ids // 128).astype(F32)
    low = (rows == ids % 128).astype(F32)
    counts[...] = lax.dot_general(high, low, (((1,), (1,)), ((), ())), preferred_element_type=F32)
    table_in.wait()

    def add_block(b, acc):
        block = tabv[:, pl.ds(pl.multiple_of(b * 128, 128), 128)].astype(F32)
        return acc + block * counts[pl.ds(b, 1), :]

    total = lax.fori_loop(0, 128, add_block, jnp.zeros((48, 128), F32), unroll=8)
    feature = jnp.sum(total, axis=1, keepdims=True) * (1.0 / PROMPT)
    first = jnp.minimum(48 * tm // 128, 10) * 128
    spot = lax.broadcasted_iota(jnp.int32, (48, 256), 0) + (48 * tm - first)
    lanes = lax.broadcasted_iota(jnp.int32, (48, 256), 1)
    placed = jnp.sum(jnp.where(spot == lanes, feature, 0.0), axis=0, keepdims=True)
    mine[0, :, :] = placed

    @pl.when(var == 0)
    def _():
        mine[1, :, :] = placed

    @pl.when(var != 0)
    def _():
        pl.semaphore_wait(barrier, 18)

    @pl.when(var == 0)
    def _():
        pl.semaphore_wait(barrier, 49)

    @pl.when(var == 0)
    def _():
        for k in range(1, 16):
            remote(mine.at[0], mine.at[1], p0s.at[k], p0r.at[0], {"var": k, "tm": tm}).start()

    for copy in weights_in:
        copy.wait()

    rel = (x, xm, xp, xq)

    def own_sends(p):
        for device, side in ((x_right, 0), (x_left, 1)):
            send(full(p, own, c), full(p, own, c), xs.at[p, side], xr.at[p, side], device)
            sent(full(p, own, c), xs.at[p, side])
        edge_sends(p, 0)
        pair_send(p, 0)

    def edge_sends(p, i):
        m = rel[i] * 2 + yh
        for d, device, edge in ((0, y_next, 3), (1, y_prev, 0)):
            blk = y_blk(p, m, c, par, d)
            send(blk, blk, ys.at[p, i, d], yr.at[p, i, d], device, yl == edge)
            sent(blk, ys.at[p, i, d])

    def pair_send(p, k):
        m = rel[k % 4] * 2 + (yh if k < 4 else 1 - yh)
        send(full(p, m, c), full(p, m, c), ss.at[p, k], sr.at[p, k], sib)
        sent(full(p, m, c), ss.at[p, k])

    def x_first(p):
        for side, i in ((0, 1), (1, 2)):
            m = rel[i] * 2 + yh
            arrived(full(p, m, c), xr.at[p, side])
            half = x_half(p, m, c, side)
            send(half, half, x2s.at[p, side], x2r.at[p, side], (x_right, x_left)[side])
            sent(half, x2s.at[p, side])
            edge_sends(p, i)
            pair_send(p, i)

    def x_second(p):
        m = xq * 2 + yh
        for side in range(2):
            arrived(x_half(p, m, c, side), x2r.at[p, side])
        edge_sends(p, 3)
        pair_send(p, 3)

    def y_step(p, i):
        m = rel[i] * 2 + (1 - yh)
        for d, device, edge in ((0, y_next, 3), (1, y_prev, 0)):
            blk = y_blk(p, m, c, par, d)
            arrived(blk, yr.at[p, i, d])
            send(blk, blk, ys.at[p, i, d], yr.at[p, i, d], device, yl != edge)
            send(blk, blk, zs.at[p, i, d], zr.at[p, i, d], (z_prev, z_next)[d])
            sent(blk, zs.at[p, i, d])

    def z_step(p, i):
        m = rel[i] * 2 + (1 - yh)
        for d in range(2):
            arrived(y_blk(p, m, c, 1 - par, d), zr.at[p, i, d])
        pair_send(p, 4 + i)

    def pair_wait(p):
        for k in range(8):
            m = rel[k % 4] * 2 + (yh if k < 4 else 1 - yh)
            arrived(full(p, m, 1 - c), sr.at[p, k])

    def scatter():
        @pl.when(var == 0)
        def _():
            for k in range(16):
                m, cc = k // 2, k % 2
                cols = pl.ds(cc * HD, HD)
                if k:
                    remote(
                        lats.at[pl.ds(32 * m, 32), cols], sp.at[m, cc, pl.ds(0, 32)], s0s.at[0, k], s0r.at[0], {"var": k, "tm": tm}
                    ).start()
                remote(
                    lats.at[pl.ds(16 * m, 16), cols], sp.at[m, cc, pl.ds(32, 16)], s0s.at[1, k], s0r.at[1], {"var": k, "tm": (tm + 31) % 32}
                ).start()
            pltpu.make_async_copy(lats.at[pl.ds(0, 32), pl.ds(0, HD)], sp.at[0, 0, pl.ds(0, 32)], loc.at[7]).start()

    def source_first():
        @pl.when(var == 0)
        def _():
            pltpu.make_async_copy(lats.at[pl.ds(0, 32), pl.ds(0, HD)], sp.at[0, 0, pl.ds(0, 32)], loc.at[7]).wait()

        @pl.when(var != 0)
        def _():
            arrived(sp.at[own, c, pl.ds(0, 32)], s0r.at[0])

        arrived(sp.at[own, c, pl.ds(32, 16)], s0r.at[1])
        send(sp.at[own, c], sp.at[own, c], s1s.at[0], s1r.at[0], partner)
        sent(sp.at[own, c], s1s.at[0])
        for side, device in ((0, x_right), (1, x_left)):
            send(sp.at[own, c], sp.at[own, c], s2s.at[0, side], s2r.at[0, side], device)
            sent(sp.at[own, c], s2s.at[0, side])

    def source_second():
        m = x * 2 + (1 - yh)
        arrived(sp.at[m, c], s1r.at[0])
        for side, device in ((0, x_right), (1, x_left)):
            send(sp.at[m, c], sp.at[m, c], s2s.at[1, side], s2r.at[1, side], device)
            sent(sp.at[m, c], s2s.at[1, side])

    def source_third():
        for side, i in ((0, 1), (1, 2)):
            m = rel[i] * 2
            for half in range(2):
                hh = yh if half == 0 else 1 - yh
                arrived(sp.at[m + hh, c], s2r.at[half, side])
            blk = sp.at[m + side, c]
            send(blk, blk, s3s.at[side], s3r.at[side], (x_right, x_left)[side])
            sent(blk, s3s.at[side])

    def source_fourth():
        for side in range(2):
            arrived(sp.at[xq * 2 + side, c], s3r.at[side])
        send(sp.at[:, c], sp.at[:, c], s4s.at[0], s4r.at[0], sib)
        sent(sp.at[:, c], s4s.at[0])

    def source_done():
        arrived(sp.at[:, 1 - c], s4r.at[0])

    def pooled_first():
        @pl.when(var != 0)
        def _():
            arrived(mine.at[1], p0r.at[0])

        keep = pltpu.make_async_copy(mine, pooled.at[yl, z], loc.at[8])
        keep.start()
        for k in range(1, NZ):
            send(mine, pooled.at[yl, z], p1s.at[k], p1r.at[k], at(x, yh, c, (z + k) % NZ, yl))
            sent(mine, p1s.at[k])
        keep.wait()

    def pooled_second():
        for k in range(1, NZ):
            arrived(pooled.at[yl, (z + NZ - k) % NZ], p1r.at[k])
        for k in range(1, NL):
            send(pooled.at[yl], pooled.at[yl], p2s.at[k], p2r.at[k], at(x, yh, c, z, (yl + k) % NL))
            sent(pooled.at[yl], p2s.at[k])

    def pooled_third():
        for k in range(1, NL):
            arrived(pooled.at[(yl + NL - k) % NL], p2r.at[k])

    own_sends(QP)
    scatter()
    seam_rows = xw.at[pl.ds(CH, SEAM)]
    send(lats.at[pl.ds(0, SEAM)], seam_rows, seam_s.at[0], seam_r.at[0], tm_prev)
    sent(lats.at[pl.ds(0, SEAM)], seam_s.at[0])
    pooled_first()
    own_sends(KP)
    x_first(QP)
    pooled_second()
    own_sends(VP)
    source_first()
    x_first(KP)
    x_second(QP)
    y_step(QP, 0)
    own_sends(OP)
    source_second()
    for i in range(1, 4):
        y_step(QP, i)
    x_second(KP)
    for i in range(4):
        z_step(QP, i)
    x_first(VP)
    source_third()
    pooled_third()
    for i in range(4):
        y_step(KP, i)
    x_second(VP)
    source_fourth()
    for i in range(4):
        z_step(KP, i)
    x_first(OP)
    for i in range(4):
        y_step(VP, i)
    x_second(OP)
    for i in range(4):
        z_step(VP, i)
    for i in range(4):
        y_step(OP, i)
    for i in range(4):
        z_step(OP, i)
    latent_in.wait()
    arrived(seam_rows, seam_r.at[0])
    source_done()

    cond = embedded[...] + jnp.zeros((1, D), F32)
    pieces_own = [cond[:, 128 * t:128 * (t + 1)] for t in range(12)]
    pieces_src = list(pieces_own)
    for t in range(32):
        first_tile = window_tile(t)
        got = pooled[t % NL, t // NL, 0], pooled[t % NL, t // NL, 1]
        for w in range(2):
            pieces_own[first_tile + w] = pieces_own[first_tile + w] + got[0][:, 128 * w:128 * (w + 1)]
            pieces_src[first_tile + w] = pieces_src[first_tile + w] + got[1][:, 128 * w:128 * (w + 1)]
    gain_own = 1.0 + jnp.concatenate(pieces_own, axis=1)
    gain_src = 1.0 + jnp.concatenate(pieces_src, axis=1)
    for r in range(WIN // 32):
        values = xw[pl.ds(32 * r, 32), :].astype(F32)
        inv = lax.rsqrt(jnp.mean(values * values, axis=-1, keepdims=True) + EPS)
        xn[pl.ds(32 * r, 32), :] = (values * inv * gain_own).astype(BF16)
    for m in range(8):
        values = jnp.concatenate([sp[m, 0], sp[m, 1]], axis=1).astype(F32)
        inv = lax.rsqrt(jnp.mean(values * values, axis=-1, keepdims=True) + EPS)
        rows_out = (values * inv * gain_src).astype(BF16)
        xn[pl.ds(WIN + 32 * m, 32), :] = rows_out[0:32]
        xn[pl.ds(WIN + CH + 16 * m, 16), :] = rows_out[32:48]

    def project(p, t, lo, hi, dst, scale=None):
        w = wqkv[p, :, :, :, pl.ds(256 * t, 256)].reshape(D, 256)
        got = jnp.dot(xn[lo:hi, :], w, preferred_element_type=F32)
        if scale is not None:
            got = got.astype(BF16).astype(F32) * scale
        dst[lo:hi, pl.ds(256 * t, 256)] = got.astype(BF16)

    pair_wait(QP)
    for t in range(3):
        project(QP, t, 0, WIN, q_s, 0.125)
    pair_wait(KP)
    for t in range(3):
        project(KP, t, 0, WIN, k_s)
        project(KP, t, WIN, 2 * WIN, k_s)
    pair_wait(VP)
    for t in range(3):
        project(VP, t, 0, WIN, v_s)
        project(VP, t, WIN, 2 * WIN, v_s)

    beyond = jnp.where(tm == 31, -1e30, 0.0)
    bias = [[(block_table[i, j].astype(F32) - 1.0) * 1e30 for j in range(3)] for i in range(3)]
    for i in range(3):
        bias[i][2] = bias[i][2] + beyond
    lane = lax.broadcasted_iota(jnp.int32, (WIN, 128), 1)
    ramp = (lax.broadcasted_iota(jnp.int32, (SEAM, 128), 0).astype(F32) + 0.5) * (1.0 / SEAM)
    lead_weight = jnp.where(tm == 0, 1.0, ramp)
    ones = jnp.ones((2 * WIN, 128), BF16)

    def head_pair(h, carry):
        cols = pl.ds(pl.multiple_of(h * 128, 128), 128)
        keys = k_s[:, cols]
        values = jnp.concatenate([v_s[:, cols], ones], axis=1)
        queries = q_s[:, cols]
        heads = []
        for e in range(2):
            masked = jnp.where((lane < 64) if e == 0 else (lane >= 64), queries, jnp.zeros_like(queries))
            s_s[e] = lax.dot_general(masked, keys, (((1,), (1,)), ((), ())), preferred_element_type=F32)
        for e in range(2):
            for i in range(3):
                r = pl.ds(128 * i, 128)
                tops = [jnp.maximum(s_s[e, r, pl.ds(128 * j, 128)], s_s[e, r, pl.ds(128 * (j + 3), 128)]) + bias[i][j] for j in range(3)]
                top = jnp.max(jnp.maximum(jnp.maximum(tops[0], tops[1]), tops[2]), axis=-1, keepdims=True)
                for j in range(6):
                    p_s[e, r, pl.ds(128 * j, 128)] = jnp.exp(s_s[e, r, pl.ds(128 * j, 128)] - (top - bias[i][j % 3])).astype(BF16)
            both = jnp.dot(p_s[e], values, preferred_element_type=F32)
            heads.append(both[:, :128] / both[:, 128:])
        attended = jnp.where(lane < 64, heads[0], heads[1])
        tail_out[:, cols] = (attended[CH:] * (1.0 - ramp)).astype(BF16)
        blended[0:SEAM, cols] = attended[0:SEAM] * lead_weight
        blended[SEAM:CH, cols] = attended[SEAM:CH]
        return carry

    lax.fori_loop(0, 6, head_pair, 0)

    send(tail_out, tail_in, tail_s.at[0], tail_r.at[0], tm_next)
    sent(tail_out, tail_s.at[0])
    pair_wait(OP)
    noise_in.wait()
    arrived(tail_in, tail_r.at[0])
    carried = jnp.where(tm == 0, 0.0, tail_in[...].astype(F32))
    mixed = jnp.concatenate([blended[0:SEAM] + carried, blended[SEAM:CH]], axis=0).astype(BF16)
    for t in range(6):
        cols = pl.ds(256 * t, 256)
        w = wo[:, :, :, cols].reshape(HD, 256)
        prediction = jnp.dot(mixed, w, preferred_element_type=F32)
        result = coefs[0] * xw[0:CH, cols].astype(F32) + coefs[1] * prediction + coefs[2] * noise_v[:, cols].astype(F32)
        out[0, :, cols] = result.astype(BF16)

    for src, ssem, _ in pending:
        remote(src, src, ssem, ssem, sib).wait_send()

    @pl.when(var == 0)
    def _():
        for k in range(16):
            if k:
                remote(mine.at[0], mine.at[1], p0s.at[k], p0r.at[0], sib).wait_send()
                blk = sp.at[0, 0, pl.ds(0, 32)]
                remote(blk, blk, s0s.at[0, k], s0r.at[0], sib).wait_send()
            blk = sp.at[0, 0, pl.ds(32, 16)]
            remote(blk, blk, s0s.at[1, k], s0r.at[1], sib).wait_send()


def local(latent, fresh_noise, timestep, prompt_ids, block_table, prompt_table, w_query, w_keyval, w_out):
    current, coef_latent, coef_pred, spread = coefficients(timestep)
    embedded = time_embedding(current)[None, :]
    coefs = jnp.stack([coef_latent, coef_pred, spread])
    anywhere = pl.BlockSpec(memory_space=pl.ANY)
    vmem = pl.BlockSpec(memory_space=pltpu.VMEM)
    smem = pl.BlockSpec(memory_space=pltpu.SMEM)
    dma = pltpu.SemaphoreType.DMA
    return pl.pallas_call(
        kernel,
        out_shape=jax.ShapeDtypeStruct((1, CH, D), BF16),
        in_specs=[anywhere, anywhere, vmem, smem, smem, vmem, anywhere, anywhere, anywhere, anywhere],
        out_specs=vmem,
        scratch_shapes=[
            pltpu.VMEM((3, 8, 2, 96, HD), BF16),
            pltpu.VMEM((8, 2, 48, D), BF16),
            pltpu.VMEM((WIN, D), BF16),
            pltpu.VMEM((8, 2, 48, HD), BF16),
            pltpu.VMEM((2 * WIN, D), BF16),
            pltpu.VMEM((48, 16384), BF16),
            pltpu.VMEM((128, 128), F32),
            pltpu.VMEM((2, 1, 256), F32),
            pltpu.VMEM((NL, NZ, 2, 1, 256), F32),
            pltpu.VMEM((WIN, HD), BF16),
            pltpu.VMEM((2 * WIN, HD), BF16),
            pltpu.VMEM((2 * WIN, HD), BF16),
            pltpu.VMEM((2, WIN, 2 * WIN), F32),
            pltpu.VMEM((2, WIN, 2 * WIN), BF16),
            pltpu.VMEM((CH, HD), F32),
            pltpu.VMEM((SEAM, HD), BF16),
            pltpu.VMEM((SEAM, HD), BF16),
            pltpu.VMEM((CH, D), BF16),
            dma((9,)),
            dma((4, 2)), dma((4, 2)), dma((4, 2)), dma((4, 2)),
            dma((4, 4, 2)), dma((4, 4, 2)), dma((4, 4, 2)), dma((4, 4, 2)),
            dma((4, 8)), dma((4, 8)),
            dma((2, 16)), dma((2,)), dma((1,)), dma((1,)), dma((2, 2)), dma((2, 2)), dma((2,)), dma((2,)), dma((1,)), dma((1,)),
            dma((1,)), dma((1,)), dma((1,)), dma((1,)),
            dma((16,)), dma((1,)), dma((NZ,)), dma((NZ,)), dma((NL,)), dma((NL,)),
        ],
        compiler_params=pltpu.CompilerParams(collective_id=0, has_side_effects=True, vmem_limit_bytes=60 * 1024 * 1024),
    )(latent, fresh_noise, embedded, coefs, block_table, prompt_ids, prompt_table.T, w_query, w_keyval, w_out)


def solution(mesh):
    placed = (
        P("var", "tm", None),
        P("var", "tm", None),
        P(),
        P("var", None),
        P(),
        P(None, "tm"),
        P("var", None),
        P("var", None),
        P("var", None),
    )
    return jax.shard_map(local, mesh=mesh, in_specs=placed, out_specs=P("var", "tm", None), check_vma=False)
```

time: 449 us -> 363 us (0.81)
  the two profiles are of different devices: /device:TPU:1 before, /device:TPU:46 now
where the time goes in v1:
time: 363 us
  Pallas kernels  358 us (99%)
    pallas_call x1, Pallas kernels, local(): pl.pallas_call(kernel, out_shape=jax.ShapeDtypeStruct((1, CH, D), BF16),...  358 us

profile of v1, /device:TPU:46, one launch (start us, length us, event | category | flops | bytes accessed | tf_op | source)
XLA Modules:
  0.0 362.6 jit_solution(16779075905344287439)
XLA Ops:
  1.2 0.6 pad_maximum_fusion.1.coefs
  1.9 0.6 broadcast_in_dim.3.embedded
  2.5 358.1 %shard_map.91 = bf16[1,256,1536]{2,1,0:T(8,128)(2,1)} custom-call(bf16[1,256,1536]{2,1,0:T(8,128)(2,1)} %latent.1, bf16[1,256,1536]{2,1,0:T(8,128)(2,1)} %noise.1, f32[1,1536]{1,0:T(1,128)} %broadcast_in_dim.3.embedded, f32[3]{0:T(128)} %pad_maximum_fusion.1.coefs, s32[3,3]{1,0:T(4,128)} %block_table.1, s32[1,64]{1,0:T(1,128)} %prompt_ids.1, ...), custom_call_target="tpu_custom_call" | custom-call | tf_op jit(solution)/shard_map/pallas_call | solution.py:476
  360.5 2.1 copy.12
  (2 shorter events, 0.1 us)

commit v2 on v1

--- a/solution.py
+++ b/solution.py
@@ -20,6 +20,7 @@
 TSTEPS = 1000
 STRIDE = 200
 NX, NZ, NL = 4, 8, 4
+LAG = 3
 EPS = 1e-06
 QP, KP, VP, OP = 0, 1, 2, 3
 
@@ -53,7 +54,7 @@
 def kernel(
     latent, noise, embedded, coefs, block_table, prompt_ids, table, w_query, w_keyval, w_out,
     out,
-    wqkv, wo, xw, sp, xn, tabv, counts, mine, pooled, q_s, k_s, v_s, s_s, p_s, blended, tail_out, tail_in, noise_v,
+    wts, xw, sp, xn, tabv, counts, mine, pooled, q_s, k_s, v_s, s_s, p_s, blended, tail_out, tail_in, noise_v,
     loc, xs, xr, x2s, x2r, ys, yr, zs, zr, ss, sr,
     s0s, s0r, s1s, s1r, s2s, s2r, s3s, s3r, s4s, s4r, seam_s, seam_r, tail_s, tail_r,
     p0s, p0r, p1s, p1r, p2s, p2r,
@@ -117,22 +118,26 @@
 
     own = x * 2 + yh
     lats = latent.at[0]
-    inputs = (w_query, w_keyval.at[:, pl.ds(0, HD)], w_keyval.at[:, pl.ds(HD, HD)], w_out)
+    inputs = (
+        (w_query, (QP, own, c)),
+        (w_keyval.at[:, pl.ds(0, HD)], (KP, own, c)),
+        (w_keyval.at[:, pl.ds(HD, HD)], (VP, own, c)),
+        (w_out.at[:, pl.ds(0, HD)], (OP, own, c, pl.ds(0, 48))),
+        (w_out.at[:, pl.ds(HD, HD)], (OP, own, c, pl.ds(48, 48))),
+    )
 
     def full(p, m, cc):
-        return wo.at[m, cc] if p == OP else wqkv.at[p, m, cc]
+        return wts.at[p, m, cc]
 
     def x_half(p, m, cc, h):
-        return wo.at[m, cc, :, pl.ds(h * 768, 768)] if p == OP else wqkv.at[p, m, cc, pl.ds(h * 48, 48), :]
+        return wts.at[p, m, cc, pl.ds(h * 48, 48), :]
 
     def y_blk(p, m, cc, pr, d):
-        if p == OP:
-            return wo.at[m, cc, :, pl.ds(pl.multiple_of(pr * 768 + d * 384, 128), 384)]
-        return wqkv.at[p, m, cc, pl.ds(pl.multiple_of(pr * 48, 16), 48), pl.ds(d * 384, 384)]
+        return wts.at[p, m, cc, pl.ds(pl.multiple_of(pr * 48, 16), 48), pl.ds(d * 384, 384)]
 
     table_in = pltpu.make_async_copy(table, tabv, loc.at[0])
     table_in.start()
-    weights_in = [pltpu.make_async_copy(inputs[p], full(p, own, c), loc.at[1 + p]) for p in range(4)]
+    weights_in = [pltpu.make_async_copy(src, wts.at[spot_], loc.at[9 + k]) for k, (src, spot_) in enumerate(inputs)]
     for copy in weights_in:
         copy.start()
     latent_in = pltpu.make_async_copy(lats, xw.at[pl.ds(0, CH)], loc.at[5])
@@ -179,7 +184,7 @@
     for copy in weights_in:
         copy.wait()
 
-    rel = (x, xm, xp, xq)
+    rel = (x, xp, xm, xq)
 
     def own_sends(p):
         for device, side in ((x_right, 0), (x_left, 1)):
@@ -201,7 +206,7 @@
         sent(full(p, m, c), ss.at[p, k])
 
     def x_first(p):
-        for side, i in ((0, 1), (1, 2)):
+        for side, i in ((0, 2), (1, 1)):
             m = rel[i] * 2 + yh
             arrived(full(p, m, c), xr.at[p, side])
             half = x_half(p, m, c, side)
@@ -217,18 +222,31 @@
         edge_sends(p, 3)
         pair_send(p, 3)
 
-    def y_step(p, i):
-        m = rel[i] * 2 + (1 - yh)
-        for d, device, edge in ((0, y_next, 3), (1, y_prev, 0)):
-            blk = y_blk(p, m, c, par, d)
-            arrived(blk, yr.at[p, i, d])
-            send(blk, blk, ys.at[p, i, d], yr.at[p, i, d], device, yl != edge)
-            send(blk, blk, zs.at[p, i, d], zr.at[p, i, d], (z_prev, z_next)[d])
-            sent(blk, zs.at[p, i, d])
+    def y_item(n, d):
+        p, i = n // 4, n % 4
+        off = i + i // 2 - 2 * (i // 3)
+        m = ((x + off) % NX) * 2 + (1 - yh)
+        blk = y_blk(p, m, c, par, d)
+        arrived(blk, yr.at[p, i, d])
+        send(blk, blk, ys.at[p, i, d], yr.at[p, i, d], (y_next, y_prev)[d], yl != (3, 0)[d])
+        send(blk, blk, zs.at[p, i, d], zr.at[p, i, d], (z_prev, z_next)[d])
+
+    def tick(t):
+        for d in range(2):
+            n = t - LAG * (1 + yl) if d == 0 else t - LAG * (4 - yl)
+            if 4 * LAG <= t <= 15 + LAG:
+                y_item(n, d)
+            elif LAG <= t <= 15 + 4 * LAG:
+                @pl.when(jnp.logical_and(n >= 0, n < 16))
+                def _():
+                    y_item(n, d)
+        if t >= 5 * LAG:
+            z_step((t - 5 * LAG) // 4, (t - 5 * LAG) % 4)
 
     def z_step(p, i):
         m = rel[i] * 2 + (1 - yh)
         for d in range(2):
+            sent(y_blk(p, m, c, par, d), zs.at[p, i, d])
             arrived(y_blk(p, m, c, 1 - par, d), zr.at[p, i, d])
         pair_send(p, 4 + i)
 
@@ -276,7 +294,7 @@
             sent(sp.at[m, c], s2s.at[1, side])
 
     def source_third():
-        for side, i in ((0, 1), (1, 2)):
+        for side, i in ((0, 2), (1, 1)):
             m = rel[i] * 2
             for half in range(2):
                 hh = yh if half == 0 else 1 - yh
@@ -317,128 +335,143 @@
         for k in range(1, NL):
             arrived(pooled.at[(yl + NL - k) % NL], p2r.at[k])
 
-    own_sends(QP)
-    scatter()
     seam_rows = xw.at[pl.ds(CH, SEAM)]
-    send(lats.at[pl.ds(0, SEAM)], seam_rows, seam_s.at[0], seam_r.at[0], tm_prev)
-    sent(lats.at[pl.ds(0, SEAM)], seam_s.at[0])
-    pooled_first()
-    own_sends(KP)
-    x_first(QP)
-    pooled_second()
-    own_sends(VP)
-    source_first()
-    x_first(KP)
-    x_second(QP)
-    y_step(QP, 0)
-    own_sends(OP)
-    source_second()
-    for i in range(1, 4):
-        y_step(QP, i)
-    x_second(KP)
-    for i in range(4):
-        z_step(QP, i)
-    x_first(VP)
-    source_third()
-    pooled_third()
-    for i in range(4):
-        y_step(KP, i)
-    x_second(VP)
-    source_fourth()
-    for i in range(4):
-        z_step(KP, i)
-    x_first(OP)
-    for i in range(4):
-        y_step(VP, i)
-    x_second(OP)
-    for i in range(4):
-        z_step(VP, i)
-    for i in range(4):
-        y_step(OP, i)
-    for i in range(4):
-        z_step(OP, i)
-    latent_in.wait()
-    arrived(seam_rows, seam_r.at[0])
-    source_done()
-
-    cond = embedded[...] + jnp.zeros((1, D), F32)
-    pieces_own = [cond[:, 128 * t:128 * (t + 1)] for t in range(12)]
-    pieces_src = list(pieces_own)
-    for t in range(32):
-        first_tile = window_tile(t)
-        got = pooled[t % NL, t // NL, 0], pooled[t % NL, t // NL, 1]
-        for w in range(2):
-            pieces_own[first_tile + w] = pieces_own[first_tile + w] + got[0][:, 128 * w:128 * (w + 1)]
-            pieces_src[first_tile + w] = pieces_src[first_tile + w] + got[1][:, 128 * w:128 * (w + 1)]
-    gain_own = 1.0 + jnp.concatenate(pieces_own, axis=1)
-    gain_src = 1.0 + jnp.concatenate(pieces_src, axis=1)
-    for r in range(WIN // 32):
-        values = xw[pl.ds(32 * r, 32), :].astype(F32)
-        inv = lax.rsqrt(jnp.mean(values * values, axis=-1, keepdims=True) + EPS)
-        xn[pl.ds(32 * r, 32), :] = (values * inv * gain_own).astype(BF16)
-    for m in range(8):
-        values = jnp.concatenate([sp[m, 0], sp[m, 1]], axis=1).astype(F32)
-        inv = lax.rsqrt(jnp.mean(values * values, axis=-1, keepdims=True) + EPS)
-        rows_out = (values * inv * gain_src).astype(BF16)
-        xn[pl.ds(WIN + 32 * m, 32), :] = rows_out[0:32]
-        xn[pl.ds(WIN + CH + 16 * m, 16), :] = rows_out[32:48]
-
-    def project(p, t, lo, hi, dst, scale=None):
-        w = wqkv[p, :, :, :, pl.ds(256 * t, 256)].reshape(D, 256)
-        got = jnp.dot(xn[lo:hi, :], w, preferred_element_type=F32)
-        if scale is not None:
-            got = got.astype(BF16).astype(F32) * scale
-        dst[lo:hi, pl.ds(256 * t, 256)] = got.astype(BF16)
-
-    pair_wait(QP)
-    for t in range(3):
-        project(QP, t, 0, WIN, q_s, 0.125)
-    pair_wait(KP)
-    for t in range(3):
-        project(KP, t, 0, WIN, k_s)
-        project(KP, t, WIN, 2 * WIN, k_s)
-    pair_wait(VP)
-    for t in range(3):
-        project(VP, t, 0, WIN, v_s)
-        project(VP, t, WIN, 2 * WIN, v_s)
+
+    def seam_send():
+        send(lats.at[pl.ds(0, SEAM)], seam_rows, seam_s.at[0], seam_r.at[0], tm_prev)
+        sent(lats.at[pl.ds(0, SEAM)], seam_s.at[0])
+
+    def gain(which):
+        parts = [1.0 + embedded[:, pl.ds(128 * t, 128)] for t in range(12)]
+        for t in range(32):
+            first_tile = window_tile(t)
+            got = pooled[t % NL, t // NL, which]
+            for w in range(2):
+                parts[first_tile + w] = parts[first_tile + w] + got[:, 128 * w:128 * (w + 1)]
+        return jnp.concatenate(parts, axis=1)
+
+    def normalize_own():
+        latent_in.wait()
+        arrived(seam_rows, seam_r.at[0])
+        own_gain = gain(0)
+        for r in range(WIN // 32):
+            values = xw[pl.ds(32 * r, 32), :].astype(F32)
+            inv = lax.rsqrt(jnp.mean(values * values, axis=-1, keepdims=True) + EPS)
+            xn[pl.ds(32 * r, 32), :] = (values * inv * own_gain).astype(BF16)
+
+    def normalize_source():
+        source_gain = gain(1)
+        for m in range(8):
+            values = jnp.concatenate([sp[m, 0], sp[m, 1]], axis=1).astype(F32)
+            inv = lax.rsqrt(jnp.mean(values * values, axis=-1, keepdims=True) + EPS)
+            rows_out = (values * inv * source_gain).astype(BF16)
+            xn[pl.ds(WIN + 32 * m, 32), :] = rows_out[0:32]
+            xn[pl.ds(WIN + CH + 16 * m, 16), :] = rows_out[32:48]
+
+    def project(p, lo, hi):
+        dst = (q_s, k_s, v_s)[p]
+        for t in range(3):
+            w = wts[p, :, :, :, pl.ds(256 * t, 256)].reshape(D, 256)
+            got = jnp.dot(xn[lo:hi, :], w, preferred_element_type=F32).astype(BF16)
+            if p == QP:
+                got = (got.astype(F32) * 0.125).astype(BF16)
+            dst[lo:hi, pl.ds(256 * t, 256)] = got
 
     beyond = jnp.where(tm == 31, -1e30, 0.0)
     bias = [[(block_table[i, j].astype(F32) - 1.0) * 1e30 for j in range(3)] for i in range(3)]
     for i in range(3):
         bias[i][2] = bias[i][2] + beyond
-    lane = lax.broadcasted_iota(jnp.int32, (WIN, 128), 1)
+
+    def soften(lo, hi):
+        def head_pair(h, carry):
+            cols = pl.ds(pl.multiple_of(h * 128, 128), 128)
+            lane = lax.broadcasted_iota(jnp.int32, (WIN, 128), 1)
+            keys = k_s[:, cols]
+            queries = q_s[:, cols]
+            for e in range(2):
+                masked = jnp.where((lane < 64) if e == 0 else (lane >= 64), queries, jnp.zeros_like(queries))
+                s_s[e] = lax.dot_general(masked, keys, (((1,), (1,)), ((), ())), preferred_element_type=F32)
+            for e in range(2):
+                for i in range(3):
+                    r = pl.ds(128 * i, 128)
+                    tops = [jnp.maximum(s_s[e, r, pl.ds(128 * j, 128)], s_s[e, r, pl.ds(128 * (j + 3), 128)]) + bias[i][j] for j in range(3)]
+                    top = jnp.max(jnp.maximum(jnp.maximum(tops[0], tops[1]), tops[2]), axis=-1, keepdims=True)
+                    for j in range(6):
+                        p_s[h, i, e, :, pl.ds(128 * j, 128)] = jnp.exp(s_s[e, r, pl.ds(128 * j, 128)] - (top - bias[i][j % 3])).astype(BF16)
+            return carry
+
+        lax.fori_loop(lo, hi, head_pair, 0)
+
+    def weighted(h, lo, hi):
+        cols = pl.ds(pl.multiple_of(h * 128, 128), 128)
+        values = jnp.concatenate([v_s[:, cols], jnp.ones((2 * WIN, 128), BF16)], axis=1)
+        both = jnp.dot(p_s[h, lo:hi].reshape((hi - lo) * 256, 2 * WIN), values, preferred_element_type=F32)
+        both = (both[:, :128] / both[:, 128:]).reshape(hi - lo, 2, 128, 128)
+        lane = lax.broadcasted_iota(jnp.int32, (128, 128), 1)
+        return cols, [jnp.where(lane < 64, both[i, 0], both[i, 1]) for i in range(hi - lo)]
+
     ramp = (lax.broadcasted_iota(jnp.int32, (SEAM, 128), 0).astype(F32) + 0.5) * (1.0 / SEAM)
     lead_weight = jnp.where(tm == 0, 1.0, ramp)
-    ones = jnp.ones((2 * WIN, 128), BF16)
-
-    def head_pair(h, carry):
-        cols = pl.ds(pl.multiple_of(h * 128, 128), 128)
-        keys = k_s[:, cols]
-        values = jnp.concatenate([v_s[:, cols], ones], axis=1)
-        queries = q_s[:, cols]
-        heads = []
-        for e in range(2):
-            masked = jnp.where((lane < 64) if e == 0 else (lane >= 64), queries, jnp.zeros_like(queries))
-            s_s[e] = lax.dot_general(masked, keys, (((1,), (1,)), ((), ())), preferred_element_type=F32)
-        for e in range(2):
-            for i in range(3):
-                r = pl.ds(128 * i, 128)
-                tops = [jnp.maximum(s_s[e, r, pl.ds(128 * j, 128)], s_s[e, r, pl.ds(128 * (j + 3), 128)]) + bias[i][j] for j in range(3)]
-                top = jnp.max(jnp.maximum(jnp.maximum(tops[0], tops[1]), tops[2]), axis=-1, keepdims=True)
-                for j in range(6):
-                    p_s[e, r, pl.ds(128 * j, 128)] = jnp.exp(s_s[e, r, pl.ds(128 * j, 128)] - (top - bias[i][j % 3])).astype(BF16)
-            both = jnp.dot(p_s[e], values, preferred_element_type=F32)
-            heads.append(both[:, :128] / both[:, 128:])
-        attended = jnp.where(lane < 64, heads[0], heads[1])
-        tail_out[:, cols] = (attended[CH:] * (1.0 - ramp)).astype(BF16)
-        blended[0:SEAM, cols] = attended[0:SEAM] * lead_weight
-        blended[SEAM:CH, cols] = attended[SEAM:CH]
-        return carry
-
-    lax.fori_loop(0, 6, head_pair, 0)
-
+
+    def tails():
+        def head_pair(h, carry):
+            cols, (last,) = weighted(h, 2, 3)
+            tail_out[:, cols] = (last * (1.0 - ramp)).astype(BF16)
+            return carry
+
+        lax.fori_loop(0, 6, head_pair, 0)
+
+    def bodies():
+        def head_pair(h, carry):
+            cols, (lead, rest) = weighted(h, 0, 2)
+            blended[0:SEAM, cols] = lead * lead_weight
+            blended[SEAM:CH, cols] = rest
+            return carry
+
+        lax.fori_loop(0, 6, head_pair, 0)
+
+    last = 16 + 5 * LAG
+    steps = {t: [] for t in range(last)}
+
+    def put(t, *step):
+        steps[t].append(step)
+
+    for p in range(4):
+        put(4 * p + 1, x_first, p)
+        put(4 * p + 3, x_second, p)
+    put(1, own_sends, VP)
+    put(3, own_sends, OP)
+    put(6, pooled_second)
+    put(12, pooled_third)
+    put(14, source_first)
+    put(17, source_second)
+    put(21, source_third)
+    put(25, source_fourth)
+    put(18, normalize_own)
+    put(21, pair_wait, QP)
+    put(21, project, QP, 0, WIN)
+    put(25, pair_wait, KP)
+    put(25, project, KP, 0, WIN)
+    put(28, source_done)
+    put(28, normalize_source)
+    put(29, project, KP, WIN, 2 * WIN)
+    own_sends(QP)
+    seam_send()
+    own_sends(KP)
+    pooled_first()
+    scatter()
+    for t in range(last):
+        for step in steps[t]:
+            step[0](*step[1:])
+        tick(t)
+    soften(0, 6)
+    pair_wait(VP)
+    project(VP, 0, WIN)
+    project(VP, WIN, 2 * WIN)
+    tails()
     send(tail_out, tail_in, tail_s.at[0], tail_r.at[0], tm_next)
     sent(tail_out, tail_s.at[0])
+    bodies()
     pair_wait(OP)
     noise_in.wait()
     arrived(tail_in, tail_r.at[0])
@@ -446,7 +479,7 @@
     mixed = jnp.concatenate([blended[0:SEAM] + carried, blended[SEAM:CH]], axis=0).astype(BF16)
     for t in range(6):
         cols = pl.ds(256 * t, 256)
-        w = wo[:, :, :, cols].reshape(HD, 256)
+        w = wts[OP, :, :, pl.ds(48 * (t // 3), 48), pl.ds(256 * (t % 3), 256)].reshape(HD, 256)
         prediction = jnp.dot(mixed, w, preferred_element_type=F32)
         result = coefs[0] * xw[0:CH, cols].astype(F32) + coefs[1] * prediction + coefs[2] * noise_v[:, cols].astype(F32)
         out[0, :, cols] = result.astype(BF16)
@@ -479,8 +512,7 @@
         in_specs=[anywhere, anywhere, vmem, smem, smem, vmem, anywhere, anywhere, anywhere, anywhere],
         out_specs=vmem,
         scratch_shapes=[
-            pltpu.VMEM((3, 8, 2, 96, HD), BF16),
-            pltpu.VMEM((8, 2, 48, D), BF16),
+            pltpu.VMEM((4, 8, 2, 96, HD), BF16),
             pltpu.VMEM((WIN, D), BF16),
             pltpu.VMEM((8, 2, 48, HD), BF16),
             pltpu.VMEM((2 * WIN, D), BF16),
@@ -492,12 +524,12 @@
             pltpu.VMEM((2 * WIN, HD), BF16),
             pltpu.VMEM((2 * WIN, HD), BF16),
             pltpu.VMEM((2, WIN, 2 * WIN), F32),
-            pltpu.VMEM((2, WIN, 2 * WIN), BF16),
+            pltpu.VMEM((6, 3, 2, 128, 2 * WIN), BF16),
             pltpu.VMEM((CH, HD), F32),
             pltpu.VMEM((SEAM, HD), BF16),
             pltpu.VMEM((SEAM, HD), BF16),
             pltpu.VMEM((CH, D), BF16),
-            dma((9,)),
+            dma((14,)),
             dma((4, 2)), dma((4, 2)), dma((4, 2)), dma((4, 2)),
             dma((4, 4, 2)), dma((4, 4, 2)), dma((4, 4, 2)), dma((4, 4, 2)),
             dma((4, 8)), dma((4, 8)),

time: 363 us -> 91.4 us (0.25)
  the two profiles are of different devices: /device:TPU:46 before, /device:TPU:1 now
where the time goes in v2:
time: 91.4 us; the launch traced here: 89.8 us
  Pallas kernels  85.3 us (93%)
  local copies, waits for them, and re-layouts  2.67 us (3%)
  between operations  1.25 us (1%)
    pallas_call x1, Pallas kernels, local(): pl.pallas_call(kernel, out_shape=jax.ShapeDtypeStruct((1, CH, D), BF16),...  85.3 us
    unnamed x1, local copies, waits for them, and re-layouts  2.06 us

profile of v2, /device:TPU:1, one launch (start us, length us, event | category | flops | bytes accessed | tf_op | source)
XLA Modules:
  0.0 89.8 jit_solution(6943030586885132240)
XLA Ops:
  1.2 0.6 pad_maximum_fusion.1.coefs
  1.9 0.6 broadcast_in_dim.3.embedded
  2.5 85.3 %shard_map.91 = bf16[1,256,1536]{2,1,0:T(8,128)(2,1)} custom-call(bf16[1,256,1536]{2,1,0:T(8,128)(2,1)} %latent.1, bf16[1,256,1536]{2,1,0:T(8,128)(2,1)} %noise.1, f32[1,1536]{1,0:T(1,128)} %broadcast_in_dim.3.embedded, f32[3]{0:T(128)} %pad_maximum_fusion.1.coefs, s32[3,3]{1,0:T(4,128)} %block_table.1, s32[1,64]{1,0:T(1,128)} %prompt_ids.1, ...), custom_call_target="tpu_custom_call" | custom-call | tf_op jit(solution)/shard_map/pallas_call | solution.py:509
  87.8 2.1 %copy.12 = bf16[1,256,1536]{2,1,0:T(8,128)(2,1)} copy(bf16[1,256,1536]{2,1,0:T(8,128)(2,1)} %shard_map.91) | data formatting | bytes 1572864
  (2 shorter events, 0.1 us)

commit v3 on v2

--- a/solution.py
+++ b/solution.py
@@ -368,9 +368,9 @@
             xn[pl.ds(WIN + 32 * m, 32), :] = rows_out[0:32]
             xn[pl.ds(WIN + CH + 16 * m, 16), :] = rows_out[32:48]
 
-    def project(p, lo, hi):
+    def project(p, lo, hi, tiles=(0, 1, 2)):
         dst = (q_s, k_s, v_s)[p]
-        for t in range(3):
+        for t in tiles:
             w = wts[p, :, :, :, pl.ds(256 * t, 256)].reshape(D, 256)
             got = jnp.dot(xn[lo:hi, :], w, preferred_element_type=F32).astype(BF16)
             if p == QP:
@@ -383,24 +383,26 @@
         bias[i][2] = bias[i][2] + beyond
 
     def soften(lo, hi):
+        count = 128 * (hi - lo)
+
         def head_pair(h, carry):
             cols = pl.ds(pl.multiple_of(h * 128, 128), 128)
-            lane = lax.broadcasted_iota(jnp.int32, (WIN, 128), 1)
+            lane = lax.broadcasted_iota(jnp.int32, (count, 128), 1)
             keys = k_s[:, cols]
-            queries = q_s[:, cols]
+            queries = q_s[128 * lo:128 * hi, cols]
             for e in range(2):
                 masked = jnp.where((lane < 64) if e == 0 else (lane >= 64), queries, jnp.zeros_like(queries))
-                s_s[e] = lax.dot_general(masked, keys, (((1,), (1,)), ((), ())), preferred_element_type=F32)
+                s_s[e, 0:count] = lax.dot_general(masked, keys, (((1,), (1,)), ((), ())), preferred_element_type=F32)
             for e in range(2):
-                for i in range(3):
-                    r = pl.ds(128 * i, 128)
+                for i in range(lo, hi):
+                    r = pl.ds(128 * (i - lo), 128)
                     tops = [jnp.maximum(s_s[e, r, pl.ds(128 * j, 128)], s_s[e, r, pl.ds(128 * (j + 3), 128)]) + bias[i][j] for j in range(3)]
                     top = jnp.max(jnp.maximum(jnp.maximum(tops[0], tops[1]), tops[2]), axis=-1, keepdims=True)
                     for j in range(6):
                         p_s[h, i, e, :, pl.ds(128 * j, 128)] = jnp.exp(s_s[e, r, pl.ds(128 * j, 128)] - (top - bias[i][j % 3])).astype(BF16)
             return carry
 
-        lax.fori_loop(lo, hi, head_pair, 0)
+        lax.fori_loop(0, 6, head_pair, 0)
 
     def weighted(h, lo, hi):
         cols = pl.ds(pl.multiple_of(h * 128, 128), 128)
@@ -449,12 +451,15 @@
     put(25, source_fourth)
     put(18, normalize_own)
     put(21, pair_wait, QP)
-    put(21, project, QP, 0, WIN)
+    for k in range(3):
+        put(21 + k, project, QP, 0, WIN, (k,))
     put(25, pair_wait, KP)
-    put(25, project, KP, 0, WIN)
+    for k in range(3):
+        put(25 + k, project, KP, 0, WIN, (k,))
     put(28, source_done)
     put(28, normalize_source)
-    put(29, project, KP, WIN, 2 * WIN)
+    for k in range(3):
+        put(28 + k, project, KP, WIN, 2 * WIN, (k,))
     own_sends(QP)
     seam_send()
     own_sends(KP)
@@ -464,13 +469,14 @@
         for step in steps[t]:
             step[0](*step[1:])
         tick(t)
-    soften(0, 6)
     pair_wait(VP)
     project(VP, 0, WIN)
     project(VP, WIN, 2 * WIN)
+    soften(2, 3)
     tails()
     send(tail_out, tail_in, tail_s.at[0], tail_r.at[0], tm_next)
     sent(tail_out, tail_s.at[0])
+    soften(0, 2)
     bodies()
     pair_wait(OP)
     noise_in.wait()

time: 91.4 us -> 89.6 us (0.980); the launches traced: 89.8 us -> 89.4 us
  no operation moved by 1% of the time
where the time goes in v3:
time: 89.6 us; the launch traced here: 89.4 us
  Pallas kernels  84.9 us (95%)
  local copies, waits for them, and re-layouts  2.67 us (3%)
  between operations  1.25 us (1%)
    pallas_call x1, Pallas kernels, local(): pl.pallas_call(kernel, out_shape=jax.ShapeDtypeStruct((1, CH, D), BF16),...  84.9 us
    unnamed x1, local copies, waits for them, and re-layouts  2.06 us

profile of v3, /device:TPU:1, one launch (start us, length us, event | category | flops | bytes accessed | tf_op | source)
XLA Modules:
  0.0 89.4 jit_solution(6286039256491740021)
XLA Ops:
  1.2 0.6 pad_maximum_fusion.1.coefs
  1.9 0.6 broadcast_in_dim.3.embedded
  2.5 84.9 %shard_map.91 = bf16[1,256,1536]{2,1,0:T(8,128)(2,1)} custom-call(bf16[1,256,1536]{2,1,0:T(8,128)(2,1)} %latent.1, bf16[1,256,1536]{2,1,0:T(8,128)(2,1)} %noise.1, f32[1,1536]{1,0:T(1,128)} %broadcast_in_dim.3.embedded, f32[3]{0:T(128)} %pad_maximum_fusion.1.coefs, s32[3,3]{1,0:T(4,128)} %block_table.1, s32[1,64]{1,0:T(1,128)} %prompt_ids.1, ...), custom_call_target="tpu_custom_call" | custom-call | tf_op jit(solution)/shard_map/pallas_call | solution.py:515
  87.3 2.1 %copy.12 = bf16[1,256,1536]{2,1,0:T(8,128)(2,1)} copy(bf16[1,256,1536]{2,1,0:T(8,128)(2,1)} %shard_map.91) | data formatting | bytes 1572864
  (2 shorter events, 0.1 us)
